TPU v7x, 128 devices: a whole 4x4x4 slice. The times are simulated.
128 devices in a mesh: src: 32 (over y, z, core), rcv: 4 (over x).
Axes of the slice: x: 4, y: 4, z: 4, core: 2. Of those that a mesh axis runs over, the one named last changes fastest.
Arguments:
- traces: bfloat16 [262144, 2048], P(('src', 'rcv'))
- trace_source: int32 [262144], P(('src', 'rcv')), may hold values from 0 to 255, as said below
- trace_offset: int32 [262144], P(('src', 'rcv')), may hold values from 0 to 63
- trace_slot: int32 [262144], P(('src', 'rcv')), may hold values from 0 to 1023, as said below
- request_list: int32 [128, 128, 8], P(('src', 'rcv')), may hold values from 0 to 63, as said below
- source_terms: float32 [256, 1024], P('src'), may hold values from -3 to 3
- receiver_terms: float32 [8192, 1024], P(('src', 'rcv')), may hold values from -3 to 3
- offset_terms: float32 [64, 1024], replicated, may hold values from -3 to 3
Outputs:
- source_new: float32 [256, 1024], P('src')
- receiver_new: float32 [8192, 1024], P(('src', 'rcv'))
- offset_new: float32 [64, 1024], replicated
Inputs may be any that keep to these rules, and one draw needn't show every extreme that they name: `trace_source`: trace t's source is one of the 8 sources of the src index that holds t. `request_list`: within one device's list for one owner the 8 entries are distinct. `trace_slot`: a slot names an owner and a position in the holding device's own request list.
All inputs are finite; a program needn't handle non-finite values.
Results may differ from a plain program's by a relative error of at most 0.0023.
Values sent between devices are 32-bit elements; how exact they have to be, the bound alone decides.
A program may use at most 128 MiB of HBM per device.

v0:
```python
import math
import jax
import jax.numpy as jnp
from jax import lax
from jax.sharding import PartitionSpec as P


def dft_table(samples):
    freq = samples // 2
    index_n = lax.broadcasted_iota(jnp.int32, (samples, freq), 0)
    index_f = lax.broadcasted_iota(jnp.int32, (samples, freq), 1)
    phase = (index_n * index_f % samples).astype(jnp.float32) * (2.0 * math.pi / samples)
    taper = 0.5 - 0.5 * jnp.cos((index_n.astype(jnp.float32) + 0.5) * (2.0 * math.pi / samples))
    scaled = taper / math.sqrt(samples)
    return jnp.concatenate([scaled * jnp.cos(phase), -scaled * jnp.sin(phase)], axis=1).astype(
        jnp.bfloat16
    )


def collect(one_hot, residual):
    upper = residual.astype(jnp.bfloat16)
    lower = (residual - upper.astype(jnp.float32)).astype(jnp.bfloat16)
    dims = (((0,), (0,)), ((), ()))
    first = lax.dot_general(one_hot, upper, dims, preferred_element_type=jnp.float32)
    second = lax.dot_general(one_hot, lower, dims, preferred_element_type=jnp.float32)
    return first + second


def local(
    traces,
    trace_source,
    trace_offset,
    trace_slot,
    request_list,
    source_terms,
    receiver_terms,
    offset_terms,
):
    peers = lax.axis_size(("src", "rcv"))
    slots = request_list.shape[2]
    freq = receiver_terms.shape[1]
    owned = receiver_terms.shape[0]
    requests = request_list.reshape(peers, slots)
    asked = lax.all_to_all(requests, ("src", "rcv"), split_axis=0, concat_axis=0, tiled=True)
    served = receiver_terms[asked.reshape(-1)].reshape(peers, slots, freq)
    fetched = lax.all_to_all(
        served, ("src", "rcv"), split_axis=0, concat_axis=0, tiled=True
    ).reshape(peers * slots, freq)
    table = dft_table(traces.shape[1])
    spectra = jnp.dot(traces, table, preferred_element_type=jnp.float32)
    real_part = spectra[:, :freq]
    imag_part = spectra[:, freq:]
    logamp = 0.5 * jnp.log(real_part * real_part + imag_part * imag_part + 0.01)
    num_src = source_terms.shape[0]
    num_off = offset_terms.shape[0]
    src_local = trace_source - lax.axis_index("src") * num_src
    residual = logamp - source_terms[src_local] - fetched[trace_slot] - offset_terms[trace_offset]
    ones = jnp.ones((traces.shape[0],), jnp.float32)
    rcv_part = jax.ops.segment_sum(residual, trace_slot, num_segments=peers * slots).reshape(
        peers, slots, freq
    )
    rcv_cnt = jax.ops.segment_sum(ones, trace_slot, num_segments=peers * slots).reshape(
        peers, slots
    )
    got_part, got_cnt = (
        lax.all_to_all(rcv_part, ("src", "rcv"), split_axis=0, concat_axis=0, tiled=True),
        lax.all_to_all(rcv_cnt, ("src", "rcv"), split_axis=0, concat_axis=0, tiled=True),
    )
    flat_asked = asked.reshape(-1)
    rcv_grad = jax.ops.segment_sum(
        got_part.reshape(peers * slots, freq), flat_asked, num_segments=owned
    )
    rcv_total = jax.ops.segment_sum(got_cnt.reshape(peers * slots), flat_asked, num_segments=owned)
    receiver_new = receiver_terms + rcv_grad / (rcv_total + 1.0)[:, None]
    columns = jnp.arange(num_src + num_off, dtype=jnp.int32)[None, :]
    both_hot = (
        (src_local[:, None] == columns) | ((trace_offset + num_src)[:, None] == columns)
    ).astype(jnp.bfloat16)
    joint = collect(both_hot, residual)
    joint_cnt = jnp.sum(both_hot.astype(jnp.float32), axis=0)
    src_part = joint[:num_src]
    off_part = joint[num_src:]
    src_cnt = joint_cnt[:num_src]
    off_cnt = joint_cnt[num_src:]
    src_sum, src_tot = lax.psum((src_part, src_cnt), "rcv")
    off_sum, off_tot = lax.psum((off_part, off_cnt), ("src", "rcv"))
    source_new = source_terms + src_sum / (src_tot + 1.0)[:, None]
    offset_new = offset_terms + off_sum / (off_tot + 1.0)[:, None]
    return (source_new, receiver_new, offset_new)


def solution(mesh):
    return jax.shard_map(
        local,
        mesh=mesh,
        in_specs=(
            P(("src", "rcv"), None),
            P(("src", "rcv")),
            P(("src", "rcv")),
            P(("src", "rcv")),
            P(("src", "rcv"), None, None),
            P("src", None),
            P(("src", "rcv"), None),
            P(),
        ),
        out_specs=(P("src", None), P(("src", "rcv"), None), P()),
        check_vma=False,
    )
```

profile of v0, /device:TPU:1, one launch (start us, length us, event | category | flops | bytes accessed | tf_op | source)
XLA Modules:
  0.0 526.6 jit_solution(12145871328240511562)
XLA Ops:
  8.6 11.5 %all-to-all-start = ((s32[128,1,8]{2,1,0:T(1,128)}), s32[128,1,8]{2,1,0:T(1,128)S(1)}, u32[]{:S(2)}, u32[]{:S(2)}) async-start(s32[128,1,8]{2,1,0:T(1,128)} %bitcast.1), calls=%async_computation | async-start | bytes 131072 | tf_op jit(solution)/shard_map/all_to_all | solution.py:44
  21.7 14.8 %scatter_custom_fusion.2 = f32[1024]{0:T(1024)S(1)} fusion(s32[2048]{0:T(1024)} %param.11, f32[2048]{0:T(1024)S(1)} %broadcast.70, f32[]{:T(128)} %constant.12.clone.1), kind=kCustom, calls=%fused_computation.67 | custom fusion | flops 2048 | bytes 4608 | tf_op jit(solution)/shard_map/scatter-add | solution.py:62
  37.2 9.8 %gather_fusion = f32[2048,1024]{1,0:T(8,128)} fusion(f32[8,1024]{1,0:T(8,128)S(1)} %copy-done, s32[2048]{0:T(1024)S(1)} %get-tuple-element.5), kind=kCustom, calls=%fused_computation | custom fusion | bytes 16785408 | tf_op jit(solution)/shard_map/gather | solution.py:57
  47.0 9.2 %copy.26 = f32[2048,1024]{0,1:T(8,128)} copy(f32[2048,1024]{1,0:T(8,128)} %gather_fusion) | data formatting | bytes 16777216 | tf_op jit(solution)/shard_map/gather | solution.py:57
  56.2 9.8 %gather_fusion.3 = f32[2048,1024]{1,0:T(8,128)} fusion(f32[64,1024]{1,0:T(8,128)S(1)} %copy-done.1, s32[2048]{0:T(1024)S(1)} %get-tuple-element.11), kind=kCustom, calls=%fused_computation.3 | custom fusion | bytes 16785408 | tf_op jit(solution)/shard_map/gather | solution.py:57
  66.0 9.2 %copy.29 = f32[2048,1024]{0,1:T(8,128)} copy(f32[2048,1024]{1,0:T(8,128)} %gather_fusion.3) | data formatting | bytes 16777216 | tf_op jit(solution)/shard_map/gather | solution.py:57
  76.6 5.4 %gather_fusion.1 = f32[1024,1024]{1,0:T(8,128)} fusion(f32[64,1024]{1,0:T(8,128)S(1)} %copy-done.2, s32[1024]{0:T(1024)S(1)} %broadcast_clamp_fusion), kind=kCustom, calls=%fused_computation.1 | custom fusion | bytes 8392704 | tf_op jit(solution)/shard_map/gather | solution.py:45
  82.1 10.2 %all-to-all-start.1 = ((f32[128,8,1024]{2,1,0:T(8,128)}), f32[128,8,1024]{2,1,0:T(8,128)}, u32[]{:S(2)}, u32[]{:S(2)}) async-start(f32[128,8,1024]{2,1,0:T(8,128)} %bitcast.14), calls=%async_computation.1 | async-start | bytes 8388608 | tf_op jit(solution)/shard_map/all_to_all | solution.py:46
  92.3 34.8 %multiply_convert_fusion = (bf16[2048,1024]{1,0:T(8,128)(2,1)S(1)}, bf16[2048,1024]{1,0:T(8,128)(2,1)S(1)}) fusion(f32[2048]{0:T(1024)S(1)} %fusion.39, f32[2048]{0:T(1024)S(1)} %subtract_multiply_fusion), kind=kLoop, calls=%fused_computation.28 | loop fusion | flops 37748736 | bytes 8404992 | tf_op jit(solution)/shard_map/convert.1
  127.0 21.9 %convolution_bitcast_fusion = f32[2048,2048]{0,1:T(8,128)} fusion(bf16[2048,2048]{1,0:T(8,128)(2,1)} %param.8, bf16[2048,1024]{1,0:T(8,128)(2,1)S(1)} %get-tuple-element.9, bf16[2048,1024]{1,0:T(8,128)(2,1)S(1)} %get-tuple-element.10), kind=kOutput, calls=%fused_computation.11 | convolution fusion | flops 17196646400 | bytes 33554432 | tf_op jit(solution)/shard_map/dot_general | solution.py:50
  149.0 9.8 %all-to-all-start.3 = ((f32[128,1,8]{2,1,0:T(1,128)}), f32[128,1,8]{2,1,0:T(1,128)S(1)}, u32[]{:S(2)}, u32[]{:S(2)}) async-start(f32[128,1,8]{2,1,0:T(1,128)} %bitcast.7), calls=%async_computation.3 | async-start | bytes 131072 | tf_op jit(solution)/shard_map/all_to_all | solution.py:67
  158.8 13.9 %gather_fusion.2 = f32[2048,1024]{1,0:T(8,128)} fusion(f32[1024,1024]{1,0:T(8,128)} %bitcast.4, s32[2048]{0:T(1024)S(1)} %fusion.37), kind=kCustom, calls=%fused_computation.2 | custom fusion | bytes 16785408 | tf_op jit(solution)/shard_map/gather | solution.py:57
  172.6 9.1 %copy.28 = f32[2048,1024]{0,1:T(8,128)} copy(f32[2048,1024]{1,0:T(8,128)} %gather_fusion.2) | data formatting | bytes 16777216 | tf_op jit(solution)/shard_map/gather | solution.py:57
  181.7 19.4 %fusion.9 = f32[2048,1024]{0,1:T(8,128)} fusion(f32[2048,1024]{0,1:T(8,128)} %copy.29, f32[2048,1024]{0,1:T(8,128)} %copy.28, f32[2048,1024]{0,1:T(8,128)} %copy.26, f32[2048,2048]{0,1:T(8,128)} %convolution_bitcast_fusion), kind=kLoop, calls=%fused_computation.22 | loop fusion | flops 16777216 | bytes 50331648 | tf_op jit(solution)/shard_map/sub | solution.py:57
  201.1 9.3 %copy.30 = f32[2048,1024]{1,0:T(8,128)} copy(f32[2048,1024]{0,1:T(8,128)} %fusion.9) | data formatting | bytes 16777216 | tf_op jit(solution)/shard_map/sub | solution.py:57
  210.4 21.2 %scatter_custom_fusion = f32[1024,1024]{1,0:T(8,128)} fusion(s32[2048]{0:T(1024)} %param.11, f32[2048,1024]{1,0:T(8,128)} %copy.30, f32[]{:T(128)} %constant.12.clone.1), kind=kCustom, calls=%fused_computation.36 | custom fusion | flops 2097152 | bytes 4194816 | tf_op jit(solution)/shard_map/scatter-add | solution.py:59
  231.5 10.2 %all-to-all-start.2 = ((f32[128,8,1024]{2,1,0:T(8,128)}), f32[128,8,1024]{2,1,0:T(8,128)}, u32[]{:S(2)}, u32[]{:S(2)}) async-start(f32[128,8,1024]{2,1,0:T(8,128)} %bitcast.15), calls=%async_computation.2 | async-start | bytes 8388608 | tf_op jit(solution)/shard_map/all_to_all | solution.py:66
  242.1 103.8 %psum.31 = f32[64]{0:T(128)S(1)} all-reduce(f32[64]{0:T(128)S(1)} %slice.23), channel_id=1, replica_groups=mesh['src'=32,'rcv'=4] {'src','rcv'}, use_global_device_ids=true, to_apply=%region_8.9 | all-reduce | flops 64 | bytes 512 | tf_op jit(solution)/shard_map/psum | solution.py:86
  347.4 7.8 %scatter_custom_fusion.3 = f32[64]{0:T(128)S(1)} fusion(s32[1024]{0:T(1024)S(1)} %reshape.116, f32[1024]{0:T(1024)S(1)} %reshape.134, f32[]{:T(128)} %constant.13.clone.1), kind=kCustom, calls=%fused_computation.70 | custom fusion | flops 1024 | bytes 260 | tf_op jit(solution)/shard_map/scatter-add | solution.py:73
  355.2 7.2 %fusion.16 = f32[72,1024]{1,0:T(8,128)S(1)} fusion(f32[2048,1024]{0,1:T(8,128)} %fusion.9, s32[2048]{0:T(1024)S(1)} %get-tuple-element.12, s32[2048]{0:T(1024)S(1)} %get-tuple-element.6), kind=kOutput, calls=%fused_computation.33 | convolution fusion | flops 310820864 | bytes 8699904 | tf_op jit(solution)/shard_map/dot_general | solution.py:25
  362.4 4.8 fusion.24
  368.0 13.2 %all-reduce = (f32[8,1024]{1,0:T(8,128)S(1)}, f32[8]{0:T(128)S(1)}) all-reduce(f32[8,1024]{1,0:T(8,128)S(1)} %slice.34, f32[8]{0:T(128)S(1)} %bitcast.18), channel_id=1, replica_groups=mesh['src'=32,'rcv'=4] {'rcv'}, use_global_device_ids=true, to_apply=%region_0.1 | all-reduce | flops 8200 | bytes 65600 | tf_op jit(solution)/shard_map/psum | solution.py:85
  381.8 125.3 %all-reduce.3.cloned.1.call-done = f32[64,1024]{1,0:T(8,128)} async-done(((f32[64,1024]{1,0:T(8,128)}), f32[64,1024]{1,0:T(8,128)}) %all-reduce.3.cloned.1.call-update) | async-done | bytes 262160 | tf_op jit(solution)/shard_map/psum | solution.py:86
  508.8 10.1 %scatter_custom_fusion.1 = f32[64,1024]{1,0:T(8,128)S(1)} fusion(s32[1024]{0:T(1024)S(1)} %reshape.116, f32[128,8,1024]{2,1,0:T(8,128)} %all-to-all-done.2, f32[]{:T(128)} %constant.12.clone.1), kind=kCustom, calls=%fused_computation.34 | custom fusion | flops 1048576 | bytes 4456452 | tf_op jit(solution)/shard_map/scatter-add | solution.py:70
  (37 shorter events, 10.9 us)
Async XLA Ops:
  7.2 30.0 %copy-start = (f32[8,1024]{1,0:T(8,128)S(1)}, f32[8,1024]{1,0:T(8,128)}, u32[]{:S(2)}) copy-start(f32[8,1024]{1,0:T(8,128)} %param.13) | copy-start | bytes 98308
  8.6 66.6 %all-to-all-start = ((s32[128,1,8]{2,1,0:T(1,128)}), s32[128,1,8]{2,1,0:T(1,128)S(1)}, u32[]{:S(2)}, u32[]{:S(2)}) async-start(s32[128,1,8]{2,1,0:T(1,128)} %bitcast.1), calls=%async_computation | async-start | bytes 131072 | tf_op jit(solution)/shard_map/all_to_all | solution.py:44
  47.0 9.2 %copy-start.1 = (f32[64,1024]{1,0:T(8,128)S(1)}, f32[64,1024]{1,0:T(8,128)}, u32[]{:S(2)}) copy-start(f32[64,1024]{1,0:T(8,128)} %param.15) | copy-start | bytes 786436
  66.0 10.6 %copy-start.2 = (f32[64,1024]{1,0:T(8,128)S(1)}, f32[64,1024]{1,0:T(8,128)}, u32[]{:S(2)}) copy-start(f32[64,1024]{1,0:T(8,128)} %param.14) | copy-start | bytes 786436
  82.1 66.9 %all-to-all-start.1 = ((f32[128,8,1024]{2,1,0:T(8,128)}), f32[128,8,1024]{2,1,0:T(8,128)}, u32[]{:S(2)}, u32[]{:S(2)}) async-start(f32[128,8,1024]{2,1,0:T(8,128)} %bitcast.14), calls=%async_computation.1 | async-start | bytes 8388608 | tf_op jit(solution)/shard_map/all_to_all | solution.py:46
  149.0 82.5 %all-to-all-start.3 = ((f32[128,1,8]{2,1,0:T(1,128)}), f32[128,1,8]{2,1,0:T(1,128)S(1)}, u32[]{:S(2)}, u32[]{:S(2)}) async-start(f32[128,1,8]{2,1,0:T(1,128)} %bitcast.7), calls=%async_computation.3 | async-start | bytes 131072 | tf_op jit(solution)/shard_map/all_to_all | solution.py:67
  231.5 277.3 %all-to-all-start.2 = ((f32[128,8,1024]{2,1,0:T(8,128)}), f32[128,8,1024]{2,1,0:T(8,128)}, u32[]{:S(2)}, u32[]{:S(2)}) async-start(f32[128,8,1024]{2,1,0:T(8,128)} %bitcast.15), calls=%async_computation.2 | async-start | bytes 8388608 | tf_op jit(solution)/shard_map/all_to_all | solution.py:66
  241.7 265.3 %all-reduce.3.cloned.1.call-start = ((), (), s32[]{:S(2)}) async-start(), calls=%async_computation.4 | async-start | bytes 524288 | tf_op jit(solution)/shard_map/psum | solution.py:86
Sparse Core Ops, SparseCore 0:
  368.1 138.9 all-reduce.2
where the time goes:
time: 528 us; the launch traced here: 527 us
  waiting for transfers between devices  125 us (24%)
  blocking collectives  117 us (22%)
  other arithmetic  115 us (22%)
  local copies, waits for them, and re-layouts  79.9 us (15%)
  starting transfers between devices  41.7 us (8%)
  matrix products  33.9 us (6%)
  between operations  14.2 us (3%)
    psum x1, waiting for transfers between devices, local(): off_sum, off_tot = lax.psum((off_part, off_cnt), ('src', 'rcv'))  125 us
    psum x1, blocking collectives, local(): off_sum, off_tot = lax.psum((off_part, off_cnt), ('src', 'rcv'))  104 us
    another operation x1, other arithmetic  34.8 us
    gather x2, local copies, waits for them, and re-layouts, local(): fetched[trace_slot]  23 us
    dot_general x1, matrix products, local(): spectra = jnp.dot(traces, table, preferred_element_type=jnp.float32)  21.9 us
    scatter-add x1, other arithmetic, local(): jax.ops.segment_sum(residual, trace_slot, num_segments=peers * slots)  21.2 us
    sub x1, other arithmetic, local(): logamp - source_terms[src_local] - fetched[trace_slot]  19.4 us
    gather x2, local copies, waits for them, and re-layouts, local(): source_terms[src_local]  19 us
  transfers between devices with their start and end apart: 5, of which 1 were waited for; matrix products, arithmetic and copies ran while one was open for 40% of the time, Pallas kernels for 0%

commit v1 on v0

--- a/solution.py
+++ b/solution.py
@@ -1,8 +1,18 @@
+import functools
 import math
 import jax
 import jax.numpy as jnp
 from jax import lax
 from jax.sharding import PartitionSpec as P
+
+
+def matrix_lift(here_x, row_axis, lane_axis):
+    for pp in (row_axis, lane_axis):
+        here_x = lax.psum(here_x, pp)
+    return here_x
+
+
+attach_the_vectors = functools.partial(matrix_lift, row_axis="rcv", lane_axis="src")
 
 
 def dft_table(samples):
@@ -83,7 +93,7 @@
     src_cnt = joint_cnt[:num_src]
     off_cnt = joint_cnt[num_src:]
     src_sum, src_tot = lax.psum((src_part, src_cnt), "rcv")
-    off_sum, off_tot = lax.psum((off_part, off_cnt), ("src", "rcv"))
+    off_sum, off_tot = attach_the_vectors((off_part, off_cnt))
     source_new = source_terms + src_sum / (src_tot + 1.0)[:, None]
     offset_new = offset_terms + off_sum / (off_tot + 1.0)[:, None]
     return (source_new, receiver_new, offset_new)

time: 528 us -> 483 us (0.915)
  waiting for transfers between devices: 125 us -> 98.1 us
  blocking collectives: 117 us -> 99.9 us
    psum x1, blocking collectives: 104 us -> 65.4 us  [matrix_lift(): here_x = lax.psum(here_x, pp)]
    psum x1 -> x2, waiting for transfers between devices: 125 us -> 98 us  [matrix_lift(): here_x = lax.psum(here_x, pp)]
    psum x1, blocking collectives: 13.2 us -> 34.5 us  [local(): src_sum, src_tot = lax.psum((src_part, src_cnt), 'rcv')]
  transfers between devices with their start and end apart: 5 -> 6, of which waited for: 1 -> 1; matrix products, arithmetic and copies ran while one was open for 40% -> 43% of each run, Pallas kernels for 0% -> 0%
where the time goes in v1:
time: 483 us; the launch traced here: 482 us
  other arithmetic  115 us (24%)
  blocking collectives  99.9 us (21%)
  waiting for transfers between devices  98.1 us (20%)
  local copies, waits for them, and re-layouts  79.9 us (17%)
  starting transfers between devices  41.8 us (9%)
  matrix products  33.9 us (7%)
  between operations  14.2 us (3%)
    psum x2, waiting for transfers between devices, matrix_lift(): here_x = lax.psum(here_x, pp)  98 us
    psum x1, blocking collectives, matrix_lift(): here_x = lax.psum(here_x, pp)  65.4 us
    another operation x1, other arithmetic  34.8 us
    psum x1, blocking collectives, local(): src_sum, src_tot = lax.psum((src_part, src_cnt), 'rcv')  34.5 us
    gather x2, local copies, waits for them, and re-layouts, local(): fetched[trace_slot]  23 us
    dot_general x1, matrix products, local(): spectra = jnp.dot(traces, table, preferred_element_type=jnp.float32)  21.9 us
    scatter-add x1, other arithmetic, local(): jax.ops.segment_sum(residual, trace_slot, num_segments=peers * slots)  21.2 us
    sub x1, other arithmetic, local(): logamp - source_terms[src_local] - fetched[trace_slot]  19.4 us
  transfers between devices with their start and end apart: 6, of which 1 were waited for; matrix products, arithmetic and copies ran while one was open for 43% of the time, Pallas kernels for 0%

profile of v1, /device:TPU:1, one launch (start us, length us, event | category | flops | bytes accessed | tf_op | source)
XLA Modules:
  0.0 482.3 jit_solution(6988393943246006110)
XLA Ops:
  8.6 11.5 %all-to-all-start = ((s32[128,1,8]{2,1,0:T(1,128)}), s32[128,1,8]{2,1,0:T(1,128)S(1)}, u32[]{:S(2)}, u32[]{:S(2)}) async-start(s32[128,1,8]{2,1,0:T(1,128)} %bitcast.1), calls=%async_computation | async-start | bytes 131072 | tf_op jit(solution)/shard_map/all_to_all | solution.py:54
  21.7 14.8 %scatter_custom_fusion.2 = f32[1024]{0:T(1024)S(1)} fusion(s32[2048]{0:T(1024)} %param.11, f32[2048]{0:T(1024)S(1)} %broadcast.70, f32[]{:T(128)} %constant.12.clone.1), kind=kCustom, calls=%fused_computation.67 | custom fusion | flops 2048 | bytes 4608 | tf_op jit(solution)/shard_map/scatter-add | solution.py:72
  37.2 9.8 %gather_fusion = f32[2048,1024]{1,0:T(8,128)} fusion(f32[8,1024]{1,0:T(8,128)S(1)} %copy-done, s32[2048]{0:T(1024)S(1)} %get-tuple-element.6), kind=kCustom, calls=%fused_computation | custom fusion | bytes 16785408 | tf_op jit(solution)/shard_map/gather | solution.py:67
  47.0 9.2 %copy.26 = f32[2048,1024]{0,1:T(8,128)} copy(f32[2048,1024]{1,0:T(8,128)} %gather_fusion) | data formatting | bytes 16777216 | tf_op jit(solution)/shard_map/gather | solution.py:67
  56.2 9.8 %gather_fusion.3 = f32[2048,1024]{1,0:T(8,128)} fusion(f32[64,1024]{1,0:T(8,128)S(1)} %copy-done.1, s32[2048]{0:T(1024)S(1)} %get-tuple-element.12), kind=kCustom, calls=%fused_computation.3 | custom fusion | bytes 16785408 | tf_op jit(solution)/shard_map/gather | solution.py:67
  66.0 9.2 %copy.29 = f32[2048,1024]{0,1:T(8,128)} copy(f32[2048,1024]{1,0:T(8,128)} %gather_fusion.3) | data formatting | bytes 16777216 | tf_op jit(solution)/shard_map/gather | solution.py:67
  76.6 5.4 %gather_fusion.1 = f32[1024,1024]{1,0:T(8,128)} fusion(f32[64,1024]{1,0:T(8,128)S(1)} %copy-done.2, s32[1024]{0:T(1024)S(1)} %broadcast_clamp_fusion), kind=kCustom, calls=%fused_computation.1 | custom fusion | bytes 8392704 | tf_op jit(solution)/shard_map/gather | solution.py:55
  82.1 10.2 %all-to-all-start.1 = ((f32[128,8,1024]{2,1,0:T(8,128)}), f32[128,8,1024]{2,1,0:T(8,128)}, u32[]{:S(2)}, u32[]{:S(2)}) async-start(f32[128,8,1024]{2,1,0:T(8,128)} %bitcast.14), calls=%async_computation.1 | async-start | bytes 8388608 | tf_op jit(solution)/shard_map/all_to_all | solution.py:56
  92.3 34.8 %multiply_convert_fusion = (bf16[2048,1024]{1,0:T(8,128)(2,1)S(1)}, bf16[2048,1024]{1,0:T(8,128)(2,1)S(1)}) fusion(f32[2048]{0:T(1024)S(1)} %fusion.39, f32[2048]{0:T(1024)S(1)} %subtract_multiply_fusion), kind=kLoop, calls=%fused_computation.28 | loop fusion | flops 37748736 | bytes 8404992 | tf_op jit(solution)/shard_map/convert.1
  127.0 21.9 %convolution_bitcast_fusion = f32[2048,2048]{0,1:T(8,128)} fusion(bf16[2048,2048]{1,0:T(8,128)(2,1)} %param.8, bf16[2048,1024]{1,0:T(8,128)(2,1)S(1)} %get-tuple-element.10, bf16[2048,1024]{1,0:T(8,128)(2,1)S(1)} %get-tuple-element.11), kind=kOutput, calls=%fused_computation.11 | convolution fusion | flops 17196646400 | bytes 33554432 | tf_op jit(solution)/shard_map/dot_general | solution.py:60
  149.0 9.8 %all-to-all-start.3 = ((f32[128,1,8]{2,1,0:T(1,128)}), f32[128,1,8]{2,1,0:T(1,128)S(1)}, u32[]{:S(2)}, u32[]{:S(2)}) async-start(f32[128,1,8]{2,1,0:T(1,128)} %bitcast.7), calls=%async_computation.3 | async-start | bytes 131072 | tf_op jit(solution)/shard_map/all_to_all | solution.py:77
  158.8 13.9 %gather_fusion.2 = f32[2048,1024]{1,0:T(8,128)} fusion(f32[1024,1024]{1,0:T(8,128)} %bitcast.4, s32[2048]{0:T(1024)S(1)} %fusion.37), kind=kCustom, calls=%fused_computation.2 | custom fusion | bytes 16785408 | tf_op jit(solution)/shard_map/gather | solution.py:67
  172.6 9.1 %copy.28 = f32[2048,1024]{0,1:T(8,128)} copy(f32[2048,1024]{1,0:T(8,128)} %gather_fusion.2) | data formatting | bytes 16777216 | tf_op jit(solution)/shard_map/gather | solution.py:67
  181.7 19.4 %fusion.9 = f32[2048,1024]{0,1:T(8,128)} fusion(f32[2048,1024]{0,1:T(8,128)} %copy.29, f32[2048,1024]{0,1:T(8,128)} %copy.28, f32[2048,1024]{0,1:T(8,128)} %copy.26, f32[2048,2048]{0,1:T(8,128)} %convolution_bitcast_fusion), kind=kLoop, calls=%fused_computation.22 | loop fusion | flops 16777216 | bytes 50331648 | tf_op jit(solution)/shard_map/sub | solution.py:67
  201.1 9.3 %copy.30 = f32[2048,1024]{1,0:T(8,128)} copy(f32[2048,1024]{0,1:T(8,128)} %fusion.9) | data formatting | bytes 16777216 | tf_op jit(solution)/shard_map/sub | solution.py:67
  210.4 21.2 %scatter_custom_fusion = f32[1024,1024]{1,0:T(8,128)} fusion(s32[2048]{0:T(1024)} %param.11, f32[2048,1024]{1,0:T(8,128)} %copy.30, f32[]{:T(128)} %constant.12.clone.1), kind=kCustom, calls=%fused_computation.36 | custom fusion | flops 2097152 | bytes 4194816 | tf_op jit(solution)/shard_map/scatter-add | solution.py:69
  231.5 10.2 %all-to-all-start.2 = ((f32[128,8,1024]{2,1,0:T(8,128)}), f32[128,8,1024]{2,1,0:T(8,128)}, u32[]{:S(2)}, u32[]{:S(2)}) async-start(f32[128,8,1024]{2,1,0:T(8,128)} %bitcast.15), calls=%async_computation.2 | async-start | bytes 8388608 | tf_op jit(solution)/shard_map/all_to_all | solution.py:76
  243.6 7.8 %scatter_custom_fusion.3 = f32[64]{0:T(128)S(1)} fusion(s32[1024]{0:T(1024)S(1)} %reshape.116, f32[1024]{0:T(1024)S(1)} %reshape.134, f32[]{:T(128)} %constant.13.clone.1), kind=kCustom, calls=%fused_computation.70 | custom fusion | flops 1024 | bytes 260 | tf_op jit(solution)/shard_map/scatter-add | solution.py:83
  251.4 7.2 %fusion.16 = f32[72,1024]{1,0:T(8,128)S(1)} fusion(f32[2048,1024]{0,1:T(8,128)} %fusion.9, s32[2048]{0:T(1024)S(1)} %get-tuple-element.13, s32[2048]{0:T(1024)S(1)} %get-tuple-element.7), kind=kOutput, calls=%fused_computation.33 | convolution fusion | flops 310820864 | bytes 8699904 | tf_op jit(solution)/shard_map/dot_general | solution.py:35
  258.6 4.8 fusion.24
  264.2 34.5 %all-reduce = (f32[8,1024]{1,0:T(8,128)S(1)}, f32[8]{0:T(128)S(1)}, f32[64]{0:T(128)S(1)}) all-reduce(f32[8,1024]{1,0:T(8,128)S(1)} %slice.34, f32[8]{0:T(128)S(1)} %bitcast.18, f32[64]{0:T(128)S(1)} %slice.23), channel_id=1, replica_groups=mesh['src'=32,'rcv'=4] {'rcv'}, use_global_device_ids=true, to_apply=%region_0.1 | all-reduce | flops 8264 | bytes 66112 | tf_op jit(solution)/shard_map/psum | solution.py:95
  298.7 65.4 %psum.47 = f32[64]{0:T(128)S(1)} all-reduce(f32[64]{0:T(128)S(1)} %get-tuple-element.5), channel_id=1, replica_groups=mesh['src'=32,'rcv'=4] {'src'}, use_global_device_ids=true, to_apply=%region_10.11 | all-reduce | flops 64 | bytes 512 | tf_op jit(solution)/shard_map/psum | solution.py:11
  364.8 98.0 %all-reduce.6.cloned.1.call-done = f32[64,1024]{1,0:T(8,128)} async-done(((f32[64,1024]{1,0:T(8,128)}), f32[64,1024]{1,0:T(8,128)}) %all-reduce.6.cloned.1.call-update) | async-done | bytes 262160 | tf_op jit(solution)/shard_map/psum | solution.py:11
  464.5 10.1 %scatter_custom_fusion.1 = f32[64,1024]{1,0:T(8,128)S(1)} fusion(s32[1024]{0:T(1024)S(1)} %reshape.116, f32[128,8,1024]{2,1,0:T(8,128)} %all-to-all-done.2, f32[]{:T(128)} %constant.12.clone.1), kind=kCustom, calls=%fused_computation.34 | custom fusion | flops 1048576 | bytes 4456452 | tf_op jit(solution)/shard_map/scatter-add | solution.py:80
  (40 shorter events, 11.0 us)
Async XLA Ops:
  7.2 30.0 %copy-start = (f32[8,1024]{1,0:T(8,128)S(1)}, f32[8,1024]{1,0:T(8,128)}, u32[]{:S(2)}) copy-start(f32[8,1024]{1,0:T(8,128)} %param.13) | copy-start | bytes 98308
  8.6 66.6 %all-to-all-start = ((s32[128,1,8]{2,1,0:T(1,128)}), s32[128,1,8]{2,1,0:T(1,128)S(1)}, u32[]{:S(2)}, u32[]{:S(2)}) async-start(s32[128,1,8]{2,1,0:T(1,128)} %bitcast.1), calls=%async_computation | async-start | bytes 131072 | tf_op jit(solution)/shard_map/all_to_all | solution.py:54
  47.0 9.2 %copy-start.1 = (f32[64,1024]{1,0:T(8,128)S(1)}, f32[64,1024]{1,0:T(8,128)}, u32[]{:S(2)}) copy-start(f32[64,1024]{1,0:T(8,128)} %param.15) | copy-start | bytes 786436
  66.0 10.6 %copy-start.2 = (f32[64,1024]{1,0:T(8,128)S(1)}, f32[64,1024]{1,0:T(8,128)}, u32[]{:S(2)}) copy-start(f32[64,1024]{1,0:T(8,128)} %param.14) | copy-start | bytes 786436
  82.1 66.9 %all-to-all-start.1 = ((f32[128,8,1024]{2,1,0:T(8,128)}), f32[128,8,1024]{2,1,0:T(8,128)}, u32[]{:S(2)}, u32[]{:S(2)}) async-start(f32[128,8,1024]{2,1,0:T(8,128)} %bitcast.14), calls=%async_computation.1 | async-start | bytes 8388608 | tf_op jit(solution)/shard_map/all_to_all | solution.py:56
  149.0 82.5 %all-to-all-start.3 = ((f32[128,1,8]{2,1,0:T(1,128)}), f32[128,1,8]{2,1,0:T(1,128)S(1)}, u32[]{:S(2)}, u32[]{:S(2)}) async-start(f32[128,1,8]{2,1,0:T(1,128)} %bitcast.7), calls=%async_computation.3 | async-start | bytes 131072 | tf_op jit(solution)/shard_map/all_to_all | solution.py:77
  231.5 233.0 %all-to-all-start.2 = ((f32[128,8,1024]{2,1,0:T(8,128)}), f32[128,8,1024]{2,1,0:T(8,128)}, u32[]{:S(2)}, u32[]{:S(2)}) async-start(f32[128,8,1024]{2,1,0:T(8,128)} %bitcast.15), calls=%async_computation.2 | async-start | bytes 8388608 | tf_op jit(solution)/shard_map/all_to_all | solution.py:76
  241.7 123.0 %all-reduce.4.cloned.1.call-start = ((), (), s32[]{:S(2)}) async-start(), calls=%async_computation.4 | async-start | bytes 524288 | tf_op jit(solution)/shard_map/psum | solution.py:11
  264.1 198.7 %all-reduce.6.cloned.1.call-start = ((), (), s32[]{:S(2)}) async-start(), calls=%async_computation.5 | async-start | bytes 524288 | tf_op jit(solution)/shard_map/psum | solution.py:11
Sparse Core Ops, SparseCore 0:
  264.2 43.2 all-reduce.3
  364.9 97.8 all-reduce.5
